TPU v7x, 256 devices: a whole 4x4x8 slice. The times are simulated.
256 devices in a mesh: expert: 32 (over y, z), vocab: 8 (over x, core).
Axes of the slice: x: 4, y: 4, z: 8, core: 2. Of those that a mesh axis runs over, the one named last changes fastest.
Arguments:
- layer_out: bfloat16 [1024, 2048], P('expert'), may hold values from -6 to 6
- moe_input: bfloat16 [1024, 2048], P('expert'), may hold values from -6 to 6
- final_gain: float32 [2048], replicated, may hold values from 0.1 to 1.9
- head_weight: bfloat16 [2048, 98304], P(None, ('expert', 'vocab')), may hold values from -0.125 to 0.125
- clean_ids: int32 [1024], P('expert'), may hold values from 0 to 98303
- levels: int32 [1024], P('expert'), may hold values from 0 to 15
- ratio_table: float32 [16], replicated, may hold values from 0.5 to 8
- gate_weights: float32 [1024, 8], P('expert'), may hold values from 0.05 to 0.5
- expert_ids: int32 [1024, 8], P('expert'), may hold values from 0 to 63, all different within a row; in each aligned block of 32 rows (0 to 31, 32 to 63, ...) at most 8 rows name the same one
- w_gate: bfloat16 [64, 2048, 1024], P('expert', None, 'vocab'), may hold values from -0.125 to 0.125
- w_up: bfloat16 [64, 2048, 1024], P('expert', None, 'vocab'), may hold values from -0.125 to 0.125
- w_down: bfloat16 [64, 1024, 2048], P('expert', 'vocab'), may hold values from -0.1875 to 0.1875
Outputs:
- head_grad: float32 [2048, 98304], P(None, ('expert', 'vocab'))
- residual_grad: float32 [1024, 2048], P('expert', 'vocab')
- input_grad: float32 [1024, 2048], P('expert', 'vocab')
Inputs may be any that keep to these rules, and one draw needn't show every extreme that they name: `expert_ids`: the 8 experts of a row are distinct; among the 32 rows of one index of expert no expert is named by more than 8 rows.
All inputs are finite; a program needn't handle non-finite values.
Results may differ from a plain program's by a relative error of at most 0.0044.
The roundings to bfloat16 on the way count: a program that leaves them out, or rounds other values in their place, can miss the bound.
Values may be sent and summed in bfloat16 or wider, within the bound.
No kernel may reach another device: no remote copies, remote signals or barrier semaphores. Data moves between devices by JAX's collectives and lax.ppermute only.
A program may use at most 64 MiB of HBM per device.

v0:
```python
import math
import jax
import jax.numpy as jnp
from jax import lax
from jax.sharding import PartitionSpec as P

epsilon = 1e-05


def sent_to_all(shard, axis):
    peers = lax.axis_size(axis)
    return lax.all_to_all(
        jnp.broadcast_to(shard[None], (peers, *shard.shape)), axis, 0, 0, tiled=True
    )


def of_everyone(shard, axis):
    everything = sent_to_all(shard, axis)
    return jnp.sum(everything, axis=0)


def sent_together(arrays, axis, split_dim, concat_dim, along):
    ends, at = ([], 0)
    for a in arrays[:-1]:
        at += a.shape[along]
        ends.append(at)
    both = jnp.concatenate(arrays, axis=along)
    return tuple(
        jnp.split(
            lax.all_to_all(both, axis, split_axis=split_dim, concat_axis=concat_dim, tiled=True),
            ends,
            axis=along,
        )
    )


def in_one_piece(arrays, axis, dim, along):
    widths = [a.shape[along] for a in arrays]
    both = jnp.concatenate(arrays, axis=along)
    result = lax.all_gather(both, axis, axis=dim, tiled=True)
    return tuple(jnp.split(result, [sum(widths[:k]) for k in range(1, len(widths))], axis=along))


def split_up(shard, dim, peers):
    before, after = (shard.shape[:dim], shard.shape[dim + 1 :])
    return jnp.moveaxis(shard.reshape(*before, peers, -1, *after), dim, 0)


def sum_at_owner(shard, axis, dim):
    parts = split_up(shard, dim, lax.axis_size(axis))
    arrived = lax.all_to_all(parts, axis, split_axis=0, concat_axis=0, tiled=True)
    return arrived.sum(axis=0)


def on_device(
    layer_out,
    moe_input,
    final_gain,
    head_weight,
    clean_ids,
    levels,
    ratio_table,
    gate_weights,
    expert_ids,
    w_gate,
    w_up,
    w_down,
):
    rows_local, model_width = layer_out.shape
    top_count = expert_ids.shape[1]
    n_expert = lax.axis_size("expert")
    n_vocab = lax.axis_size("vocab")
    total_rows = rows_local * n_expert
    local_experts = w_gate.shape[0]
    experts_all = local_experts * n_expert
    capacity = max(2, 2 * rows_local * top_count // experts_all)
    feature_share = model_width // n_vocab
    vocab_local = head_weight.shape[1]
    values = layer_out.astype(jnp.float32)
    row_scale = jnp.sqrt(jnp.mean(values * values, axis=1, keepdims=True) + epsilon)
    unit_rows = values / row_scale
    normed = (unit_rows * final_gain[None, :]).astype(jnp.bfloat16)
    normed_all, clean_all, level_all = (
        lax.all_gather(normed, "expert", axis=0, tiled=True),
        lax.all_gather(clean_ids, "expert", axis=0, tiled=True),
        lax.all_gather(levels, "expert", axis=0, tiled=True),
    )
    level_labels = jnp.arange(ratio_table.shape[0], dtype=jnp.int32)
    ratio_rows = jnp.sum(
        jnp.where(level_all[:, None] == level_labels[None, :], ratio_table[None, :], 0.0), axis=1
    )
    column_start = (lax.axis_index("expert") * n_vocab + lax.axis_index("vocab")) * vocab_local
    columns = column_start + jnp.arange(vocab_local, dtype=jnp.int32)
    scores = jnp.dot(normed_all, head_weight, preferred_element_type=jnp.float32)
    target_hit = (clean_all[:, None] == columns[None, :]).astype(jnp.float32)
    loss_scale = 1.0 / math.sqrt(total_rows)
    score_grad = ((jnp.exp(scores) - ratio_rows[:, None] * target_hit) * loss_scale).astype(
        jnp.bfloat16
    )
    head_grad = lax.dot_general(
        normed_all, score_grad, (((0,), (0,)), ((), ())), preferred_element_type=jnp.float32
    )
    partial_grad = lax.psum_scatter(
        lax.dot_general(
            score_grad, head_weight, (((1,), (1,)), ((), ())), preferred_element_type=jnp.float32
        ),
        "expert",
        scatter_dimension=0,
        tiled=True,
    )
    normed_grad = of_everyone(partial_grad, "vocab")
    gained = final_gain[None, :] * normed_grad
    residual_full = (
        gained - unit_rows * jnp.mean(unit_rows * gained, axis=1, keepdims=True)
    ) / row_scale
    feature_start = lax.axis_index("vocab") * feature_share
    residual_grad = lax.dynamic_slice_in_dim(residual_full, feature_start, feature_share, 1)
    flat_ids = expert_ids.reshape(-1)
    labels = jnp.arange(experts_all, dtype=jnp.int32)
    onehot = (flat_ids[:, None] == labels[None, :]).astype(jnp.int32)
    earlier = jnp.cumsum(onehot, axis=0) - onehot
    slot_index = jnp.sum(earlier * onehot, axis=1)
    position = flat_ids * capacity + slot_index
    routed_grad = (
        (gate_weights[:, :, None] * residual_full[:, None, :])
        .astype(jnp.bfloat16)
        .reshape(-1, model_width)
    )
    inputs_rep = jnp.repeat(moe_input, top_count, axis=0)
    buffer_rows = experts_all * capacity
    send_inputs = (
        jnp.zeros((buffer_rows, model_width), jnp.bfloat16)
        .at[position]
        .set(inputs_rep)
        .reshape(experts_all, capacity, model_width)
    )
    send_grads = (
        jnp.zeros((buffer_rows, model_width), jnp.bfloat16)
        .at[position]
        .set(routed_grad)
        .reshape(experts_all, capacity, model_width)
    )
    part_inputs = lax.dynamic_slice_in_dim(send_inputs, feature_start, feature_share, 2)
    part_grads = lax.dynamic_slice_in_dim(send_grads, feature_start, feature_share, 2)
    moved_inputs, moved_grads = sent_together((part_inputs, part_grads), "expert", 0, 1, 2)
    inputs_slot, grads_slot = in_one_piece((moved_inputs, moved_grads), "vocab", 2, 0)
    gate_pre = jnp.einsum("esd,edf->esf", inputs_slot, w_gate, preferred_element_type=jnp.float32)
    up_pre = jnp.einsum("esd,edf->esf", inputs_slot, w_up, preferred_element_type=jnp.float32)
    act_grad = jnp.einsum("esd,efd->esf", grads_slot, w_down, preferred_element_type=jnp.float32)
    sigmoid_gate = jax.nn.sigmoid(gate_pre)
    gate_grad = (act_grad * up_pre * sigmoid_gate * (1.0 + gate_pre * (1.0 - sigmoid_gate))).astype(
        jnp.bfloat16
    )
    up_grad = (act_grad * gate_pre * sigmoid_gate).astype(jnp.bfloat16)
    partial_input = jnp.einsum(
        "esf,edf->esd", gate_grad, w_gate, preferred_element_type=jnp.float32
    )
    partial_input = partial_input + jnp.einsum(
        "esf,edf->esd", up_grad, w_up, preferred_element_type=jnp.float32
    )
    slot_share = sum_at_owner(partial_input, "vocab", 2)
    returned = lax.all_to_all(slot_share, "expert", split_axis=1, concat_axis=0, tiled=True)
    per_pair = returned.reshape(-1, feature_share)[position]
    input_grad = jnp.sum(per_pair.reshape(rows_local, top_count, feature_share), axis=1)
    return (head_grad, residual_grad, input_grad)


def solution(mesh):
    in_specs = (
        P("expert", None),
        P("expert", None),
        P(),
        P(None, ("expert", "vocab")),
        P("expert"),
        P("expert"),
        P(),
        P("expert", None),
        P("expert", None),
        P("expert", None, "vocab"),
        P("expert", None, "vocab"),
        P("expert", "vocab", None),
    )
    out_specs = (P(None, ("expert", "vocab")), P("expert", "vocab"), P("expert", "vocab"))
    return jax.shard_map(
        on_device, mesh=mesh, in_specs=in_specs, out_specs=out_specs, check_vma=False
    )
```

profile of v0, /device:TPU:32, one launch (start us, length us, event | category | flops | bytes accessed | tf_op | source)
XLA Modules:
  0.0 536.3 jit_solution(17601662020850642282)
XLA Ops:
  7.2 1.1 fusion.27
  8.4 1.7 multiply_convert_fusion.4
  10.2 1.3 dynamic-slice
  12.1 0.9 dynamic-update-slice.1
  12.9 0.8 dynamic-update-slice
  13.8 23.3 %all-reduce.2 = (s32[1024]{0:T(1024)S(1)}, s32[1024]{0:T(1024)S(1)}) all-reduce(s32[1024]{0:T(1024)S(1)} %dynamic-update-slice.1, s32[1024]{0:T(1024)S(1)} %dynamic-update-slice), channel_id=1, replica_groups=mesh['expert'=32,'vocab'=8] {'expert'}, use_global_device_ids=true, to_apply=%add.1 | all-reduce | flops 2048 | bytes 16384
  37.1 0.7 select_reduce_fusion
  37.8 58.0 %all-gather.3.cloned.1.call-done = bf16[1024,2048]{1,0:T(8,128)(2,1)} async-done(((bf16[32,2048]{1,0:T(8,128)(2,1)}), bf16[1024,2048]{1,0:T(8,128)(2,1)}) %all-gather.3.cloned.1.call-update) | async-done | bytes 4194320 | tf_op jit(solution)/shard_map/all_gather | solution.py:84
  95.8 4.5 fusion.39
  100.3 1.2 copy-done.4
  101.5 5.7 %fusion.1 = f32[1024,2048]{1,0:T(8,128)} fusion(bf16[2048,384]{1,0:T(8,128)(2,1)S(1)} %copy-done, f32[1024,384]{1,0:T(8,128)S(1)} %fusion.39, f32[1024]{0:T(1024)S(1)} %select_reduce_fusion, s32[384]{0:T(512)S(1)} %iota_add_fusion, s32[1024]{0:T(1024)S(1)} %get-tuple-element.4), kind=kOutput, calls=%fused_computation.8 | convolution fusion | flops 1612578816 | bytes 11544064 | tf_op jit(solution)/shard_map/dot_general | solution.py:104
  107.2 225.0 %reduce-scatter.2.cloned.1.call-done = f32[32,2048]{1,0:T(8,128)} async-done(((f32[1024,2048]{1,0:T(8,128)}), f32[32,2048]{1,0:T(8,128)}) %reduce-scatter.2.cloned.1.call-update) | async-done | bytes 262160 | tf_op jit(solution)/shard_map/reduce_scatter | solution.py:103
  332.2 2.5 broadcast_in_dim.18
  334.7 4.5 all-to-all-start
  339.3 0.1 eq.57
  339.6 0.1 mul.122
  339.7 0.6 reduce-window.6
  340.3 0.2 slice_reduce_fusion
  340.6 0.1 mul.124
  340.7 0.1 fusion.31
  340.9 3.7 scatter_custom_fusion
  344.6 21.8 %all-to-all-done = f32[8,32,2048]{2,1,0:T(8,128)} async-done(((f32[8,32,2048]{2,1,0:T(8,128)}), f32[8,32,2048]{2,1,0:T(8,128)}, u32[]{:S(2)}, u32[]{:S(2)}) %all-to-all-start) | async-done | bytes 2097184 | tf_op jit(solution)/shard_map/all_to_all | solution.py:12
  366.4 1.7 reduce_sum.67
  368.2 0.2 multiply_reduce_fusion
  368.4 0.1 subtract_divide_fusion
  368.5 3.8 scatter_custom_fusion.1
  372.3 1.1 constant_dynamic-slice_fusion
  373.4 25.3 %all_to_all.43 = bf16[64,8,512]{2,1,0:T(8,128)(2,1)S(1)} all-to-all(bf16[64,8,512]{2,1,0:T(8,128)(2,1)S(1)} %pad_maximum_fusion), channel_id=1, replica_groups=mesh['expert'=32,'vocab'=8] {'expert'}, dimensions={0} | all-to-all | bytes 1048576 | tf_op jit(solution)/shard_map/all_to_all | solution.py:30
  398.8 0.8 pad_maximum_fusion.1
  399.7 33.0 %all-gather.5.cloned.1.call-done = bf16[4,256,2048]{2,1,0:T(8,128)(2,1)} async-done(((bf16[4,256,256]{2,1,0:T(8,128)(2,1)}), bf16[4,256,2048]{2,1,0:T(8,128)(2,1)}) %all-gather.5.cloned.1.call-update) | async-done | bytes 4194320 | tf_op jit(solution)/shard_map/all_gather | solution.py:40
  432.6 2.7 fusion.41
  435.4 0.4 copy-done.1
  435.8 0.7 fusion.42
  436.5 0.5 copy-done.2
  437.0 0.7 fusion.7
  437.7 0.7 fusion.40
  438.4 0.7 convolution_add_fusion
  439.2 0.4 copy.57
  439.6 54.2 %all_to_all.44 = f32[8,2,256,256]{3,2,1,0:T(8,128)} all-to-all(f32[8,2,256,256]{3,2,1,0:T(8,128)S(1)} %bitcast.67), channel_id=1, replica_groups=mesh['expert'=32,'vocab'=8] {'vocab'}, dimensions={0} | all-to-all | bytes 8388608 | tf_op jit(solution)/shard_map/all_to_all | solution.py:51
  493.8 3.3 reduce_sum.71
  497.1 2.4 copy.48
  499.5 10.1 %all-to-all-start.3 = ((f32[2,256,256]{2,0,1:T(2,128)}), f32[2,256,256]{2,0,1:T(2,128)}, u32[]{:S(2)}, u32[]{:S(2)}) async-start(f32[2,256,256]{2,0,1:T(2,128)} %copy.48), calls=%async_computation.4 | async-start | bytes 1048576 | tf_op jit(solution)/shard_map/all_to_all | solution.py:162
  509.7 6.3 %fusion.2 = f32[2048,384]{1,0:T(8,128)} fusion(bf16[1024,2048]{1,0:T(8,128)(2,1)} %all-gather.3.cloned.1.call-done, f32[1024,384]{1,0:T(8,128)S(1)} %copy-done.5, f32[1024]{0:T(1024)S(1)} %select_reduce_fusion, s32[384]{0:T(512)S(1)} %iota_add_fusion, s32[1024]{0:T(1024)S(1)} %get-tuple-element.4), kind=kOutput, calls=%fused_computation.9 | convolution fusion | flops 1612578816 | bytes 8922624 | tf_op jit(solution)/shard_map/dot_general | solution.py:100
  516.0 0.6 constant_dynamic-slice_fusion.2
  516.6 10.4 %all-to-all-done.3 = f32[2,256,256]{2,0,1:T(2,128)} async-done(((f32[2,256,256]{2,0,1:T(2,128)}), f32[2,256,256]{2,0,1:T(2,128)}, u32[]{:S(2)}, u32[]{:S(2)}) %all-to-all-start.3) | async-done | bytes 524320 | tf_op jit(solution)/shard_map/all_to_all | solution.py:162
  527.0 1.1 copy.58
  528.1 1.0 gather_fusion
  529.1 0.7 bitcast_reduce_fusion
  (44 shorter events, 0.8 us)
Async XLA Ops:
  7.2 88.7 %copy-start = (bf16[2048,384]{1,0:T(8,128)(2,1)S(1)}, bf16[2048,384]{1,0:T(8,128)(2,1)}, u32[]{:S(2)}) copy-start(bf16[2048,384]{1,0:T(8,128)(2,1)} %param.15) | copy-start | bytes 4718596
  7.2 88.6 %all-gather.3.cloned.1.call-start = ((), (), s32[]{:S(2)}) async-start(), calls=%async_computation.5 | async-start | bytes 4325376 | tf_op jit(solution)/shard_map/all_gather | solution.py:84
  10.1 322.1 %reduce-scatter.2.cloned.1.call-start = ((), (), s32[]{:S(2)}) async-start(), calls=%async_computation.6 | async-start | bytes 8650752 | tf_op jit(solution)/shard_map/reduce_scatter | solution.py:103
  100.3 1.2 copy-start.4
  334.7 4.5 copy-start.9
  334.7 5.8 %copy-start.10 = (f32[32,8]{0,1:T(8,128)S(1)}, f32[32,8]{0,1:T(8,128)}, u32[]{:S(2)}) copy-start(f32[32,8]{0,1:T(8,128)} %param.19) | copy-start | bytes 3076
  334.7 6.1 %copy-start.7 = (bf16[32,2048]{1,0:T(8,128)(2,1)S(1)}, bf16[32,2048]{1,0:T(8,128)(2,1)}, u32[]{:S(2)}) copy-start(bf16[32,2048]{1,0:T(8,128)(2,1)} %param.13) | copy-start | bytes 393220
  334.7 31.7 %all-to-all-start = ((f32[8,32,2048]{2,1,0:T(8,128)}), f32[8,32,2048]{2,1,0:T(8,128)}, u32[]{:S(2)}, u32[]{:S(2)}) async-start(f32[8,32,2048]{2,1,0:T(8,128)} %broadcast_in_dim.18), calls=%async_computation.1 | async-start | bytes 4194304 | tf_op jit(solution)/shard_map/all_to_all | solution.py:12
  339.2 93.4 %all-gather.5.cloned.1.call-start = ((), (), s32[]{:S(2)}) async-start(), calls=%async_computation.7 | async-start | bytes 4718592 | tf_op jit(solution)/shard_map/all_gather | solution.py:40
  340.8 27.3 %copy-start.6 = (bf16[32,2048]{1,0:T(8,128)(2,1)S(1)}, bf16[32,2048]{1,0:T(8,128)(2,1)}, u32[]{:S(2)}) copy-start(bf16[32,2048]{1,0:T(8,128)(2,1)} %param.12) | copy-start | bytes 393220
  340.9 27.3 %copy-start.8 = (f32[2048]{0:T(1024)S(1)}, f32[2048]{0:T(1024)}, u32[]{:S(2)}) copy-start(f32[2048]{0:T(1024)} %param.14) | copy-start | bytes 24580
  399.7 35.7 %copy-start.3 = (bf16[2,2048,128]{2,1,0:T(8,128)(2,1)S(1)}, bf16[2,2048,128]{2,1,0:T(8,128)(2,1)}, u32[]{:S(2)}) copy-start(bf16[2,2048,128]{2,1,0:T(8,128)(2,1)} %param.21) | copy-start | bytes 3145732
  432.6 3.1 copy-start.1
  435.8 1.2 copy-start.2
  497.1 12.5 %copy-start.5 = (f32[1024,384]{1,0:T(8,128)S(1)}, f32[1024,384]{1,0:T(8,128)}, u32[]{:S(2)}) copy-start(f32[1024,384]{1,0:T(8,128)} %copy-done.4) | copy-start | bytes 4718596
  499.5 27.5 %all-to-all-start.3 = ((f32[2,256,256]{2,0,1:T(2,128)}), f32[2,256,256]{2,0,1:T(2,128)}, u32[]{:S(2)}, u32[]{:S(2)}) async-start(f32[2,256,256]{2,0,1:T(2,128)} %copy.48), calls=%async_computation.4 | async-start | bytes 1048576 | tf_op jit(solution)/shard_map/all_to_all | solution.py:162
Sparse Core Ops, SparseCore 0:
  11.2 84.6 all-gather.2
  107.3 224.8 reduce-scatter.1
  399.8 32.8 all-gather.4
where the time goes:
time: 537 us; the launch traced here: 536 us
  waiting for transfers between devices  348 us (65%)
  blocking collectives  103 us (19%)
  matrix products  22 us (4%)
  local copies, waits for them, and re-layouts  18.8 us (4%)
  other arithmetic  15.1 us (3%)
  starting transfers between devices  14.7 us (3%)
  between operations  14.7 us (3%)
    reduce_scatter x1, waiting for transfers between devices, on_device(): lax.psum_scatter(lax.dot_general(score_grad, head_weight, (((1,), (1,)),...  225 us
    all_gather x1, waiting for transfers between devices, on_device(): lax.all_gather(normed, 'expert', axis=0, tiled=True)  58 us
    all_to_all x1, blocking collectives, sum_at_owner(): lax.all_to_all(parts, axis, split_axis=0, concat_axis=0, tiled=True)  54.2 us
    all_gather x1, waiting for transfers between devices, in_one_piece(): result = lax.all_gather(both, axis, axis=dim, tiled=True)  33 us
    all_to_all x1, blocking collectives, sent_together(): lax.all_to_all(both, axis, split_axis=split_dim, concat_axis=concat_dim,...  25.3 us
    unnamed x1, blocking collectives  23.3 us
    all_to_all x1, waiting for transfers between devices, sent_to_all(): lax.all_to_all(jnp.broadcast_to(shard[None], (peers, *shard.shape)), axis...  21.8 us
  transfers between devices with their start and end apart: 5, of which 5 were waited for; matrix products, arithmetic and copies ran while one was open for 3% of the time, Pallas kernels for 0%

commit v1 on v0

--- a/solution.py
+++ b/solution.py
@@ -3,6 +3,7 @@
 import jax.numpy as jnp
 from jax import lax
 from jax.sharding import PartitionSpec as P
+from jax.lax import all_to_all, axis_size
 
 epsilon = 1e-05
 
@@ -81,7 +82,9 @@
     unit_rows = values / row_scale
     normed = (unit_rows * final_gain[None, :]).astype(jnp.bfloat16)
     normed_all, clean_all, level_all = (
-        lax.all_gather(normed, "expert", axis=0, tiled=True),
+        jnp.concatenate(
+            all_to_all(jnp.stack(axis_size("expert") * [normed]), "expert", 0, 0), axis=0
+        ),
         lax.all_gather(clean_ids, "expert", axis=0, tiled=True),
         lax.all_gather(levels, "expert", axis=0, tiled=True),
     )

time: 537 us -> 573 us (1.067)
  blocking collectives: 103 us -> 183 us
  waiting for transfers between devices: 348 us -> 293 us
  starting transfers between devices: 14.7 us -> 26.3 us
    unnamed x1, blocking collectives: 23.3 us -> 104 us
    all_gather x1 -> x0, waiting for transfers between devices: 58 us -> none  [on_device(): lax.all_gather(normed, 'expert', axis=0, tiled=True)]
    all_to_all x0 -> x1, starting transfers between devices: none -> 11.6 us  [on_device(): all_to_all(jnp.stack(axis_size('expert') * [normed]), 'expert', 0, 0)]
  transfers between devices with their start and end apart: 5 -> 5, of which waited for: 5 -> 4; matrix products, arithmetic and copies ran while one was open for 3% -> 2% of each run, Pallas kernels for 0% -> 0%
where the time goes in v1:
time: 573 us; the launch traced here: 572 us
  waiting for transfers between devices  293 us (51%)
  blocking collectives  183 us (32%)
  starting transfers between devices  26.3 us (5%)
  matrix products  22 us (4%)
  local copies, waits for them, and re-layouts  19.3 us (3%)
  between operations  15 us (3%)
  other arithmetic  13.8 us (2%)
    reduce_scatter x1, waiting for transfers between devices, on_device(): lax.psum_scatter(lax.dot_general(score_grad, head_weight, (((1,), (1,)),...  227 us
    unnamed x1, blocking collectives  104 us
    all_to_all x1, blocking collectives, sum_at_owner(): lax.all_to_all(parts, axis, split_axis=0, concat_axis=0, tiled=True)  54.2 us
    all_gather x1, waiting for transfers between devices, in_one_piece(): result = lax.all_gather(both, axis, axis=dim, tiled=True)  33 us
    all_to_all x1, blocking collectives, sent_together(): lax.all_to_all(both, axis, split_axis=split_dim, concat_axis=concat_dim,...  25.3 us
    all_to_all x1, waiting for transfers between devices, sent_to_all(): lax.all_to_all(jnp.broadcast_to(shard[None], (peers, *shard.shape)), axis...  21.8 us
    all_to_all x1, starting transfers between devices, on_device(): all_to_all(jnp.stack(axis_size('expert') * [normed]), 'expert', 0, 0)  11.6 us
  transfers between devices with their start and end apart: 5, of which 4 were waited for; matrix products, arithmetic and copies ran while one was open for 2% of the time, Pallas kernels for 0%

profile of v1, /device:TPU:32, one launch (start us, length us, event | category | flops | bytes accessed | tf_op | source)
XLA Modules:
  0.0 572.4 jit_solution(7072301570850568783)
XLA Ops:
  7.2 1.2 fusion.27
  8.3 1.0 multiply_convert_fusion.4
  9.4 2.5 stack.2
  11.8 11.6 %all-to-all-start = ((bf16[32,32,2048]{2,1,0:T(8,128)(2,1)}), bf16[32,32,2048]{2,1,0:T(8,128)(2,1)}, u32[]{:S(2)}, u32[]{:S(2)}) async-start(bf16[32,32,2048]{2,1,0:T(8,128)(2,1)} %stack.2), calls=%async_computation | async-start | bytes 8388608 | tf_op jit(solution)/shard_map/all_to_all | solution.py:86
  23.5 0.6 dynamic-slice
  24.7 0.2 dynamic-update-slice.1
  25.0 0.2 dynamic-update-slice
  25.2 103.9 %all-reduce.2 = (s32[1024]{0:T(1024)S(1)}, s32[1024]{0:T(1024)S(1)}) all-reduce(s32[1024]{0:T(1024)S(1)} %dynamic-update-slice.1, s32[1024]{0:T(1024)S(1)} %dynamic-update-slice), channel_id=1, replica_groups=mesh['expert'=32,'vocab'=8] {'expert'}, use_global_device_ids=true, to_apply=%add.1 | all-reduce | flops 2048 | bytes 16384
  129.3 4.5 fusion.39
  133.8 1.2 copy-done.4
  135.0 5.7 fusion.1
  140.6 227.5 %reduce-scatter.2.cloned.1.call-done = f32[32,2048]{1,0:T(8,128)} async-done(((f32[1024,2048]{1,0:T(8,128)}), f32[32,2048]{1,0:T(8,128)}) %reduce-scatter.2.cloned.1.call-update) | async-done | bytes 262160 | tf_op jit(solution)/shard_map/reduce_scatter | solution.py:106
  368.1 2.5 broadcast_in_dim.18
  370.6 4.5 all-to-all-start.1
  375.2 0.1 eq.57
  375.5 0.1 mul.122
  375.6 0.6 reduce-window.6
  376.2 0.2 slice_reduce_fusion
  376.5 0.1 mul.124
  376.6 0.1 fusion.31
  376.8 3.7 scatter_custom_fusion
  380.5 21.8 %all-to-all-done.1 = f32[8,32,2048]{2,1,0:T(8,128)} async-done(((f32[8,32,2048]{2,1,0:T(8,128)}), f32[8,32,2048]{2,1,0:T(8,128)}, u32[]{:S(2)}, u32[]{:S(2)}) %all-to-all-start.1) | async-done | bytes 2097184 | tf_op jit(solution)/shard_map/all_to_all | solution.py:13
  402.3 1.7 reduce_sum.67
  404.0 0.2 multiply_reduce_fusion
  404.3 0.1 subtract_divide_fusion
  404.4 3.8 scatter_custom_fusion.1
  408.2 1.1 constant_dynamic-slice_fusion
  409.3 25.3 %all_to_all.48 = bf16[64,8,512]{2,1,0:T(8,128)(2,1)S(1)} all-to-all(bf16[64,8,512]{2,1,0:T(8,128)(2,1)S(1)} %pad_maximum_fusion), channel_id=1, replica_groups=mesh['expert'=32,'vocab'=8] {'expert'}, dimensions={0} | all-to-all | bytes 1048576 | tf_op jit(solution)/shard_map/all_to_all | solution.py:31
  434.6 0.8 pad_maximum_fusion.1
  435.5 33.0 %all-gather.2.cloned.1.call-done = bf16[4,256,2048]{2,1,0:T(8,128)(2,1)} async-done(((bf16[4,256,256]{2,1,0:T(8,128)(2,1)}), bf16[4,256,2048]{2,1,0:T(8,128)(2,1)}) %all-gather.2.cloned.1.call-update) | async-done | bytes 4194320 | tf_op jit(solution)/shard_map/all_gather | solution.py:41
  468.5 2.7 fusion.41
  471.2 0.4 copy-done.1
  471.6 0.7 fusion.42
  472.3 0.5 copy-done.2
  472.8 0.7 fusion.7
  473.6 0.7 fusion.40
  474.3 0.7 convolution_add_fusion
  475.0 0.4 copy.57
  475.4 54.2 %all_to_all.49 = f32[8,2,256,256]{3,2,1,0:T(8,128)} all-to-all(f32[8,2,256,256]{3,2,1,0:T(8,128)S(1)} %bitcast.68), channel_id=1, replica_groups=mesh['expert'=32,'vocab'=8] {'vocab'}, dimensions={0} | all-to-all | bytes 8388608 | tf_op jit(solution)/shard_map/all_to_all | solution.py:52
  529.7 3.3 reduce_sum.71
  533.0 2.4 copy.48
  535.3 10.1 %all-to-all-start.4 = ((f32[2,256,256]{2,0,1:T(2,128)}), f32[2,256,256]{2,0,1:T(2,128)}, u32[]{:S(2)}, u32[]{:S(2)}) async-start(f32[2,256,256]{2,0,1:T(2,128)} %copy.48), calls=%async_computation.5 | async-start | bytes 1048576 | tf_op jit(solution)/shard_map/all_to_all | solution.py:165
  545.5 6.3 %fusion.2 = f32[2048,384]{1,0:T(8,128)} fusion(bf16[1024,2048]{1,0:T(8,128)(2,1)} %bitcast, f32[1024,384]{1,0:T(8,128)S(1)} %copy-done.5, f32[1024]{0:T(1024)S(1)} %select_reduce_fusion, s32[384]{0:T(512)S(1)} %iota_add_fusion, s32[1024]{0:T(1024)S(1)} %get-tuple-element.4), kind=kOutput, calls=%fused_computation.9 | convolution fusion | flops 1612578816 | bytes 8922624 | tf_op jit(solution)/shard_map/dot_general | solution.py:103
  551.8 0.6 constant_dynamic-slice_fusion.2
  552.5 10.4 %all-to-all-done.4 = f32[2,256,256]{2,0,1:T(2,128)} async-done(((f32[2,256,256]{2,0,1:T(2,128)}), f32[2,256,256]{2,0,1:T(2,128)}, u32[]{:S(2)}, u32[]{:S(2)}) %all-to-all-start.4) | async-done | bytes 524320 | tf_op jit(solution)/shard_map/all_to_all | solution.py:165
  562.8 1.1 copy.58
  564.0 1.0 gather_fusion
  564.9 0.7 bitcast_reduce_fusion
  (52 shorter events, 0.8 us)
Async XLA Ops:
  7.2 122.1 %copy-start = (bf16[2048,384]{1,0:T(8,128)(2,1)S(1)}, bf16[2048,384]{1,0:T(8,128)(2,1)}, u32[]{:S(2)}) copy-start(bf16[2048,384]{1,0:T(8,128)(2,1)} %param.15) | copy-start | bytes 4718596
  11.8 11.6 %copy-start.14 = (u32[256]{0:T(256)S(1)}, u32[256]{0:T(256)}, u32[]{:S(2)}) copy-start(u32[256]{0:T(256)} %constant.48) | copy-start | bytes 3076
  11.8 12.9 %copy-start.12 = (s32[32]{0:T(128)S(1)}, s32[32]{0:T(128)}, u32[]{:S(2)}) copy-start(s32[32]{0:T(128)} %param.17) | copy-start | bytes 388
  11.8 13.1 %copy-start.13 = (s32[32]{0:T(128)S(1)}, s32[32]{0:T(128)}, u32[]{:S(2)}) copy-start(s32[32]{0:T(128)} %param.16) | copy-start | bytes 388
  11.8 117.3 %copy-start.11 = (f32[16]{0:T(128)S(1)}, f32[16]{0:T(128)}, u32[]{:S(2)}) copy-start(f32[16]{0:T(128)} %param.18) | copy-start | bytes 196
  11.8 117.4 %all-to-all-start = ((bf16[32,32,2048]{2,1,0:T(8,128)(2,1)}), bf16[32,32,2048]{2,1,0:T(8,128)(2,1)}, u32[]{:S(2)}, u32[]{:S(2)}) async-start(bf16[32,32,2048]{2,1,0:T(8,128)(2,1)} %stack.2), calls=%async_computation | async-start | bytes 8388608 | tf_op jit(solution)/shard_map/all_to_all | solution.py:86
  23.4 344.7 %reduce-scatter.2.cloned.1.call-start = ((), (), s32[]{:S(2)}) async-start(), calls=%async_computation.6 | async-start | bytes 8650752 | tf_op jit(solution)/shard_map/reduce_scatter | solution.py:106
  133.8 1.2 copy-start.4
  370.6 4.5 copy-start.9
  370.6 5.8 %copy-start.10 = (f32[32,8]{0,1:T(8,128)S(1)}, f32[32,8]{0,1:T(8,128)}, u32[]{:S(2)}) copy-start(f32[32,8]{0,1:T(8,128)} %param.19) | copy-start | bytes 3076
  370.6 6.1 %copy-start.7 = (bf16[32,2048]{1,0:T(8,128)(2,1)S(1)}, bf16[32,2048]{1,0:T(8,128)(2,1)}, u32[]{:S(2)}) copy-start(bf16[32,2048]{1,0:T(8,128)(2,1)} %param.13) | copy-start | bytes 393220
  370.6 31.7 %all-to-all-start.1 = ((f32[8,32,2048]{2,1,0:T(8,128)}), f32[8,32,2048]{2,1,0:T(8,128)}, u32[]{:S(2)}, u32[]{:S(2)}) async-start(f32[8,32,2048]{2,1,0:T(8,128)} %broadcast_in_dim.18), calls=%async_computation.2 | async-start | bytes 4194304 | tf_op jit(solution)/shard_map/all_to_all | solution.py:13
  375.1 93.4 %all-gather.2.cloned.1.call-start = ((), (), s32[]{:S(2)}) async-start(), calls=%async_computation.7 | async-start | bytes 4718592 | tf_op jit(solution)/shard_map/all_gather | solution.py:41
  376.7 27.3 %copy-start.6 = (bf16[32,2048]{1,0:T(8,128)(2,1)S(1)}, bf16[32,2048]{1,0:T(8,128)(2,1)}, u32[]{:S(2)}) copy-start(bf16[32,2048]{1,0:T(8,128)(2,1)} %param.12) | copy-start | bytes 393220
  376.8 27.3 %copy-start.8 = (f32[2048]{0:T(1024)S(1)}, f32[2048]{0:T(1024)}, u32[]{:S(2)}) copy-start(f32[2048]{0:T(1024)} %param.14) | copy-start | bytes 24580
  435.5 35.7 %copy-start.3 = (bf16[2,2048,128]{2,1,0:T(8,128)(2,1)S(1)}, bf16[2,2048,128]{2,1,0:T(8,128)(2,1)}, u32[]{:S(2)}) copy-start(bf16[2,2048,128]{2,1,0:T(8,128)(2,1)} %param.21) | copy-start | bytes 3145732
  468.5 3.1 copy-start.1
  471.6 1.2 copy-start.2
  533.0 12.5 %copy-start.5 = (f32[1024,384]{1,0:T(8,128)S(1)}, f32[1024,384]{1,0:T(8,128)}, u32[]{:S(2)}) copy-start(f32[1024,384]{1,0:T(8,128)} %copy-done.4) | copy-start | bytes 4718596
  535.3 27.5 %all-to-all-start.4 = ((f32[2,256,256]{2,0,1:T(2,128)}), f32[2,256,256]{2,0,1:T(2,128)}, u32[]{:S(2)}, u32[]{:S(2)}) async-start(f32[2,256,256]{2,0,1:T(2,128)} %copy.48), calls=%async_computation.5 | async-start | bytes 1048576 | tf_op jit(solution)/shard_map/all_to_all | solution.py:165
Sparse Core Ops, SparseCore 0:
  140.8 227.2 reduce-scatter.1
  435.6 32.7 all-gather.1
